TPU v7x, 32 devices: a whole 2x2x4 slice. The times are simulated.
32 devices in a mesh: sub: 4 (over x, core), slab: 8 (over z, y).
Axes of the slice: x: 2, y: 2, z: 4, core: 2. Of those that a mesh axis runs over, the one named last changes fastest.
Arguments:
- source: float32 [4, 256, 256, 256], P('sub', 'slab'), may hold values from -6 to 6
- coarse: float32 [2, 4, 256, 256, 256], P(None, 'sub', 'slab'), may hold values from -4 to 4
- rho: float32 [4], replicated, may hold values from 0.3 to 45, as said below
- basis_x: float32 [256, 256], replicated, may hold values from -0.375 to 0.375
- basis_y: float32 [256, 256], replicated, may hold values from -0.375 to 0.375
- basis_z: float32 [256, 256], replicated, may hold values from -0.375 to 0.375
- eigen_x: float32 [256], replicated, may hold values from 0.1 to 3
- eigen_y: float32 [256], replicated, may hold values from 0.1 to 3
- eigen_z: float32 [256], replicated, may hold values from 0.1 to 3
- face_stiff: float32 [256, 256], replicated, may hold values from 0.2 to 2
Outputs:
- solution: float32 [4, 256, 256, 256], P('sub', 'slab')
- multipliers: float32 [4, 256, 256], P('sub', 'slab')
- jump: float32 [4, 256, 256], P('sub', 'slab')
Inputs may be any that keep to these rules, and one draw needn't show every extreme that they name: `rho`: positive coefficient of each subdomain.
All inputs are finite; a program needn't handle non-finite values.
Results may differ from a plain program's by a relative error of at most 0.00014.
Values sent between devices are 32-bit elements; how exact they have to be, the bound alone decides.
A program may use at most 128 MiB of HBM per device.

v0:
```python
import jax
import jax.numpy as jnp
from jax import lax
from jax.experimental.layout import Layout, with_layout_constraint
from jax.experimental import pallas as pl
from jax.experimental.pallas import tpu as pltpu
from jax.sharding import PartitionSpec as P

ITERS = 2
CHUNKS = 4

HI = lax.Precision.HIGHEST
MID = lax.Precision.HIGH
F32 = jnp.float32
BF16 = jnp.bfloat16


def split(value):
    top = value.astype(BF16)
    return top, (value - top.astype(F32)).astype(BF16)


def edge_kernel(part_ref, basis_ref, pair_ref, eigen_ref, first_ref, last_ref, out_ref):
    top, low = split(basis_ref[...])
    right = jnp.concatenate([top, low, top], axis=0)
    for at in range(part_ref.shape[1]):
        top, low = split(part_ref[:, at, :])
        left = jnp.concatenate([top, top, low], axis=0)
        hat = lax.dot_general(left, right, (((0,), (0,)), ((), ())), preferred_element_type=F32)
        modes = hat / (pair_ref[at : at + 1, :] + eigen_ref[...])
        width = basis_ref.shape[1]
        out_ref[at : at + 1, :width] = jnp.sum(modes * first_ref[...], axis=0, keepdims=True)
        out_ref[at : at + 1, width:] = jnp.sum(modes * last_ref[...], axis=0, keepdims=True)


def partial_edges(part, basis_rows, pair, eigen, first, last):
    rows, width, depth = part.shape
    block = 8
    whole = lambda j: (0, 0)
    return pl.pallas_call(
        edge_kernel,
        out_shape=jax.ShapeDtypeStruct((width, 2 * width), F32),
        grid=(width // block,),
        in_specs=[
            pl.BlockSpec((rows, block, depth), lambda j: (0, j, 0)),
            pl.BlockSpec((rows, width), whole),
            pl.BlockSpec((block, width), lambda j: (j, 0)),
            pl.BlockSpec((depth, width), whole),
            pl.BlockSpec((depth, width), whole),
            pl.BlockSpec((depth, width), whole),
        ],
        out_specs=pl.BlockSpec((block, 2 * width), lambda j: (j, 0)),
        compiler_params=pltpu.CompilerParams(vmem_limit_bytes=24 * 2**20),
        cost_estimate=pl.CostEstimate(
            flops=2 * width * width * depth * 96, bytes_accessed=4 * width * rows * depth, transcendentals=0
        ),
        name="partial_edges",
    )(part, basis_rows, pair, eigen, first, last)


def last_kernel(*refs):
    basis_ref, out_ref = refs[-2:]
    top, low = split(basis_ref[...])
    left = jnp.concatenate([top, top, low], axis=1)
    for at in range(out_ref.shape[0]):
        top, low = split(jnp.concatenate([ref[at] for ref in refs[:-2]], axis=0))
        right = jnp.concatenate([top, low, top], axis=0)
        out_ref[at] = jnp.dot(left, right, preferred_element_type=F32)


def last_product(fields, basis_y):
    rows, piece, depth = fields[0].shape
    width = basis_y.shape[0]
    block = 4
    return pl.pallas_call(
        last_kernel,
        out_shape=jax.ShapeDtypeStruct((rows, width, depth), F32),
        grid=(rows // block,),
        in_specs=[pl.BlockSpec((block, piece, depth), lambda x: (x, 0, 0))] * len(fields)
        + [pl.BlockSpec((width, width), lambda x: (0, 0))],
        out_specs=pl.BlockSpec((block, width, depth), lambda x: (x, 0, 0)),
        compiler_params=pltpu.CompilerParams(vmem_limit_bytes=24 * 2**20),
        name="last_product",
    )(*fields, basis_y)


def from_behind(block, axis, distance):
    count = lax.axis_size(axis)
    return lax.ppermute(block, axis, [((i - distance) % count, i) for i in range(count)])


def exchange(blocks, extra, before):
    size = blocks.shape[1]
    if extra is not None:
        blocks = jnp.concatenate([blocks, extra], axis=1)
    if before:
        blocks = with_layout_constraint(blocks, Layout(major_to_minor=(0, 1, 2, 3)))
        blocks, _ = lax.optimization_barrier((blocks, before[-1]))
    got = lax.all_to_all(blocks, "slab", split_axis=0, concat_axis=0, tiled=True)
    before.append(got)
    return got[:, :size], got[:, size:]


def face_step(apart, weight, basis_x, basis_y, face_stiff):
    subs = lax.axis_size("sub")
    jump = jnp.einsum("ji,yj->yi", apart, basis_y, precision=HI)
    jump = jnp.einsum("yi,xi->xy", jump, basis_x, precision=HI)
    face = jnp.einsum("xy,yj->xj", jump, basis_y, precision=HI)
    face = jnp.einsum("xj,xi->ij", face, basis_x, precision=HI) * face_stiff
    face = jnp.einsum("ij,xi->xj", face, basis_x, precision=HI)
    face = jnp.einsum("xj,yj->xy", face, basis_y, precision=HI)
    search = weight * face
    sums = jnp.stack([jnp.sum(jump * search), jnp.sum(search * search)])
    sums = jnp.broadcast_to(sums[:, None], (2, 128))
    total = sums
    for distance in range(1, subs):
        total = total + from_behind(sums, "sub", distance)
    return jump, search, total[0, 0] / (total[1, 0] + 1e-06)


def on_device(
    source, coarse, rho, basis_x, basis_y, basis_z, eigen_x, eigen_y, eigen_z, face_stiff
):
    field = source[0]
    rows, width = field.shape[:2]
    sub_index = lax.axis_index("sub")
    slab_index = lax.axis_index("slab")
    subs = lax.axis_size("sub")
    slabs = lax.axis_size("slab")
    own_rho = lax.dynamic_slice_in_dim(rho, sub_index, 1, 0)[0]
    next_rho = lax.dynamic_slice_in_dim(rho, (sub_index + 1) % subs, 1, 0)[0]
    weight = 0.5 * (own_rho + next_rho)
    piece = width // CHUNKS
    lot = piece // slabs
    edge_basis = jnp.stack([basis_z[0], basis_z[width - 1]])
    before = []

    part = jnp.einsum("xyz,zk->xyk", field + coarse[1, 0], basis_z, precision=MID)

    def outward(c, extra=None):
        some = jnp.einsum("xyk,yj->xjk", part, basis_y[:, c * piece : (c + 1) * piece], precision=MID)
        some = some.reshape(rows, slabs, lot, width).swapaxes(0, 1)
        some, extra = exchange(some, extra, before)
        return some.reshape(width, lot, width), extra

    lines = [outward(0)[0]]

    early = jnp.einsum("xyz,zk->xyk", field + coarse[0, 0], basis_z, precision=MID)
    early = jnp.einsum("xyk,yj->xjk", early, basis_y, precision=MID)
    spread_out = lambda column: jnp.broadcast_to(column[:, None], (width, width))
    share = partial_edges(
        early,
        lax.dynamic_slice_in_dim(basis_x, slab_index * rows, rows, 0),
        eigen_y[:, None] + eigen_x[None, :],
        spread_out(eigen_z),
        spread_out(basis_z[0]),
        spread_out(basis_z[width - 1]),
    )
    some, extra = outward(1, share.reshape(slabs, 2 * CHUNKS, lot, width))
    lines.append(some)
    edges = jnp.sum(extra, axis=0).reshape(width // slabs, 2 * width) / own_rho
    apart = edges[:, width:] - from_behind(edges[:, :width], "sub", -1)
    apart = jnp.broadcast_to(apart.reshape(1, CHUNKS, lot, width), (slabs, CHUNKS, lot, width))
    some, extra = outward(2, apart)
    lines.append(some)
    lines.append(outward(3)[0])
    _, search, alpha = face_step(extra.reshape(width, width), weight, basis_x, basis_y, face_stiff)
    multipliers = alpha * search
    pair = jnp.stack([alpha * from_behind(search, "sub", 1), -multipliers])
    pair = jnp.einsum("pxy,yj->pxj", pair, basis_y, precision=HI)
    pair = jnp.einsum("pxj,xi->pij", pair, basis_x, precision=HI)

    def modal(c):
        start = c * piece + slab_index * lot
        eigen_part = lax.dynamic_slice_in_dim(eigen_y, start, lot, 0)
        pair_part = lax.dynamic_slice_in_dim(pair, start, lot, 2)
        denom = (eigen_x[:, None, None] + eigen_part[None, :, None] + eigen_z[None, None, :]) * own_rho
        hat = jnp.einsum("xjk,xi->ijk", lines[c], basis_x, precision=MID)
        hat = hat + pair_part[0][:, :, None] * edge_basis[0] + pair_part[1][:, :, None] * edge_basis[1]
        modes = hat / denom
        spread = jnp.einsum("ijk,xi->xjk", modes, basis_x, precision=MID)
        edges = jnp.einsum("ijk,pk->pji", modes, edge_basis, precision=HI)
        return spread.reshape(slabs, rows, lot, width), edges

    def inward(spread, extra=None):
        some, extra = exchange(spread, extra, before)
        some = jnp.einsum("dxjk,zk->xdjz", some, basis_z, precision=MID)
        return some.reshape(rows, piece, width), extra

    spreads, edges = zip(*[modal(c) for c in range(CHUNKS)])
    edges = jnp.stack(edges, axis=1)
    apart = edges[1] - from_behind(edges[0], "sub", -1)
    apart = jnp.broadcast_to(apart[None], (slabs, CHUNKS, lot, width))
    fields = [inward(spreads[0])[0], inward(spreads[1])[0]]
    some, extra = inward(spreads[2], apart)
    fields.append(some)
    extra = extra.swapaxes(0, 1).reshape(width, width)
    jump, search, alpha = face_step(extra, weight, basis_x, basis_y, face_stiff)
    multipliers = multipliers + alpha * search
    own = lambda face: lax.dynamic_slice_in_dim(face, slab_index * rows, rows, 0)
    fields.append(inward(spreads[3])[0])
    solution = last_product(fields, basis_y)
    return (solution[None], own(multipliers)[None], own(jump)[None])


def solution(mesh):
    in_specs = (
        P("sub", "slab", None, None),
        P(None, "sub", "slab", None, None),
        P(),
        P(),
        P(),
        P(),
        P(),
        P(),
        P(),
        P(),
    )
    out_specs = (P("sub", "slab", None, None), P("sub", "slab", None), P("sub", "slab", None))
    return jax.shard_map(
        on_device, mesh=mesh, in_specs=in_specs, out_specs=out_specs, check_vma=False
    )
```

profile of v0, /device:TPU:8, one launch (start us, length us, event | category | flops | bytes accessed | tf_op | source)
XLA Modules:
  0.0 503.2 jit_solution(2780240705299562861)
XLA Ops:
  0.7 7.9 %fusion.1 = f32[32,256,256]{2,1,0:T(8,128)S(1)} fusion(f32[1,32,256,256]{3,2,1,0:T(8,128)} %param.10, f32[2,1,32,256,256]{4,3,2,1,0:T(8,128)} %param.11, f32[256,256]{1,0:T(8,128)} %param.15), kind=kOutput, calls=%fused_computation.3 | convolution fusion | flops 3223322624 | bytes 25427968 | tf_op jit(solution)/shard_map/xyz,zk->xyk/dot_general | solution.py:138
  8.6 2.7 convolution_bitcast_fusion.4
  11.9 1.5 copy.130
  13.5 6.6 %all-to-all-start = ((f32[8,32,8,256]{3,2,1,0:T(8,128)}), f32[8,32,8,256]{3,2,1,0:T(8,128)}, u32[]{:S(2)}, u32[]{:S(2)}) async-start(f32[8,32,8,256]{3,2,1,0:T(8,128)} %bitcast.296), calls=%async_computation | async-start | bytes 4194304 | tf_op jit(solution)/shard_map/all_to_all | solution.py:99
  20.3 7.9 %fusion = f32[32,256,256]{1,2,0:T(8,128)S(1)} fusion(f32[1,32,256,256]{3,2,1,0:T(8,128)} %param.10, f32[2,1,32,256,256]{4,3,2,1,0:T(8,128)} %param.11, f32[256,256]{1,0:T(8,128)S(1)} %copy-done.7), kind=kOutput, calls=%fused_computation.1 | convolution fusion | flops 3223322624 | bytes 25427968 | tf_op jit(solution)/shard_map/xyz,zk->xyk/dot_general | solution.py:148
  28.2 3.8 convolution_bitcast_fusion.part_ref
  32.3 48.2 %partial_edges.1 = f32[256,512]{1,0:T(8,128)S(1)} custom-call(f32[32,256,256]{2,1,0:T(8,128)S(1)} %convolution_bitcast_fusion.part_ref, f32[32,256]{1,0:T(8,128)S(1)} %constant_dynamic-slice_fusion.basis_ref, f32[256,256]{1,0:T(8,128)S(1)} %broadcast_add_fusion.pair_ref, f32[256,256]{1,0:T(8,128)S(1)} %broadcast_in_dim.26.eigen_ref, ...), custom_call_target="tpu_custom_call" | custom-call | flops 3221225472 | bytes 8388608 | tf_op jit(solution)/shard_map/partial_edges/pallas_call | solution.py:40
  80.6 6.1 %convolution_bitcast_fusion.2 = f32[32,8,8,256]{3,2,1,0:T(8,128)S(1)} fusion(f32[32,256,256]{2,1,0:T(8,128)} %copy-done.4, f32[256,256]{1,0:T(8,128)S(1)} %copy-done.1), kind=kOutput, calls=%fused_computation.41 | convolution fusion | flops 805306368 | bytes 10616832 | tf_op jit(solution)/shard_map/xyk,yj->xjk/dot_general | solution.py:141
  86.9 1.7 pad_maximum_fusion
  88.6 6.1 %all-to-all-start.1 = ((f32[8,40,8,256]{3,2,1,0:T(8,128)}), f32[8,40,8,256]{3,2,1,0:T(8,128)S(1)}, u32[]{:S(2)}, u32[]{:S(2)}) async-start(f32[8,40,8,256]{3,2,1,0:T(8,128)} %pad_maximum_fusion), calls=%async_computation.1 | async-start | bytes 5242880 | tf_op jit(solution)/shard_map/all_to_all | solution.py:99
  95.3 55.9 %all-to-all-done.1 = f32[8,40,8,256]{3,2,1,0:T(8,128)S(1)} async-done(((f32[8,40,8,256]{3,2,1,0:T(8,128)}), f32[8,40,8,256]{3,2,1,0:T(8,128)S(1)}, u32[]{:S(2)}, u32[]{:S(2)}) %all-to-all-start.1) | async-done | bytes 2621472 | tf_op jit(solution)/shard_map/all_to_all | solution.py:99
  151.9 1.4 collective-permute-start
  153.3 5.9 %convolution_bitcast_fusion.3 = f32[32,8,8,256]{3,2,1,0:T(8,128)S(1)} fusion(f32[32,256,256]{2,1,0:T(8,128)} %copy-done.4, f32[256,256]{1,0:T(8,128)S(1)} %copy-done.1), kind=kOutput, calls=%fused_computation.42 | convolution fusion | flops 805306368 | bytes 10616832 | tf_op jit(solution)/shard_map/xyk,yj->xjk/dot_general | solution.py:141
  159.5 1.6 pad_maximum_fusion.1
  161.1 6.1 %all-to-all-start.2 = ((f32[8,36,8,256]{3,2,1,0:T(8,128)}), f32[8,36,8,256]{3,2,1,0:T(8,128)}, u32[]{:S(2)}, u32[]{:S(2)}) async-start(f32[8,36,8,256]{3,2,1,0:T(8,128)} %pad_maximum_fusion.1), calls=%async_computation.2 | async-start | bytes 4718592 | tf_op jit(solution)/shard_map/all_to_all | solution.py:99
  168.5 6.1 %convolution_bitcast_fusion.1 = f32[32,8,8,256]{3,2,1,0:T(8,128)S(1)} fusion(f32[32,256,256]{2,1,0:T(8,128)} %copy-done.4, f32[256,256]{1,0:T(8,128)S(1)} %copy-done.1), kind=kOutput, calls=%fused_computation.40 | convolution fusion | flops 805306368 | bytes 10616832 | tf_op jit(solution)/shard_map/xyk,yj->xjk/dot_general | solution.py:141
  174.6 1.5 copy.127
  176.2 42.9 %all-to-all-done.2 = f32[8,36,8,256]{3,2,1,0:T(8,128)} async-done(((f32[8,36,8,256]{3,2,1,0:T(8,128)}), f32[8,36,8,256]{3,2,1,0:T(8,128)}, u32[]{:S(2)}, u32[]{:S(2)}) %all-to-all-start.2) | async-done | bytes 2359328 | tf_op jit(solution)/shard_map/all_to_all | solution.py:99
  220.7 1.3 fusion.74
  222.0 6.8 %all-to-all-start.3 = ((f32[8,32,8,256]{3,2,1,0:T(8,128)}), f32[8,32,8,256]{3,2,1,0:T(8,128)}, u32[]{:S(2)}, u32[]{:S(2)}) async-start(f32[8,32,8,256]{3,2,1,0:T(8,128)} %bitcast.303), calls=%async_computation.3 | async-start | bytes 4194304 | tf_op jit(solution)/shard_map/all_to_all | solution.py:99
  228.8 1.6 fusion.75
  230.4 1.6 fusion.31
  233.6 1.4 pad_maximum_fusion.4
  235.0 1.5 collective-permute-start.2
  236.5 1.5 collective-permute-start.3
  241.9 2.3 collective-permute-done.4
  245.6 5.0 fusion.13
  250.6 1.4 copy-done.11
  253.0 2.5 copy.52
  255.6 18.6 %all-to-all-done.3 = f32[8,32,8,256]{3,2,1,0:T(8,128)} async-done(((f32[8,32,8,256]{3,2,1,0:T(8,128)}), f32[8,32,8,256]{3,2,1,0:T(8,128)}, u32[]{:S(2)}, u32[]{:S(2)}) %all-to-all-start.3) | async-done | bytes 2097184 | tf_op jit(solution)/shard_map/all_to_all | solution.py:99
  274.2 6.8 %all-to-all-start.4 = ((f32[8,32,8,256]{3,2,1,0:T(8,128)}), f32[8,32,8,256]{3,2,1,0:T(8,128)}, u32[]{:S(2)}, u32[]{:S(2)}) async-start(f32[8,32,8,256]{3,2,1,0:T(8,128)} %bitcast.306), calls=%async_computation.4 | async-start | bytes 4194304 | tf_op jit(solution)/shard_map/all_to_all | solution.py:99
  281.2 3.5 fusion.11
  284.7 1.4 copy-done.13
  287.1 2.5 copy.58
  289.7 36.6 %all-to-all-done.4 = f32[8,32,8,256]{3,2,1,0:T(8,128)} async-done(((f32[8,32,8,256]{3,2,1,0:T(8,128)}), f32[8,32,8,256]{3,2,1,0:T(8,128)}, u32[]{:S(2)}, u32[]{:S(2)}) %all-to-all-start.4) | async-done | bytes 2097184 | tf_op jit(solution)/shard_map/all_to_all | solution.py:99
  326.3 6.4 %all-to-all-start.5 = ((f32[8,32,8,256]{3,2,1,0:T(8,128)}), f32[8,32,8,256]{3,2,1,0:T(8,128)S(1)}, u32[]{:S(2)}, u32[]{:S(2)}) async-start(f32[8,32,8,256]{3,2,1,0:T(8,128)} %bitcast.305), calls=%async_computation.5 | async-start | bytes 4194304 | tf_op jit(solution)/shard_map/all_to_all | solution.py:99
  332.7 1.9 slice.131
  337.6 3.5 fusion.9
  342.2 5.0 fusion.7
  347.2 1.4 copy-done.10
  349.8 1.3 collective-permute-start.5
  352.1 1.2 copy.62
  353.4 1.6 pad_maximum_fusion.2
  354.9 23.7 %all-to-all-done.5 = f32[8,32,8,256]{3,2,1,0:T(8,128)S(1)} async-done(((f32[8,32,8,256]{3,2,1,0:T(8,128)}), f32[8,32,8,256]{3,2,1,0:T(8,128)S(1)}, u32[]{:S(2)}, u32[]{:S(2)}) %all-to-all-start.5) | async-done | bytes 2097184 | tf_op jit(solution)/shard_map/all_to_all | solution.py:99
  378.7 1.4 copy-done.8
  380.1 6.1 %all-to-all-start.6 = ((f32[8,36,8,256]{3,2,1,0:T(8,128)}), f32[8,36,8,256]{3,2,1,0:T(8,128)S(1)}, u32[]{:S(2)}, u32[]{:S(2)}) async-start(f32[8,36,8,256]{3,2,1,0:T(8,128)} %pad_maximum_fusion.2), calls=%async_computation.6 | async-start | bytes 4718592 | tf_op jit(solution)/shard_map/all_to_all | solution.py:99
  386.2 2.6 convolution_bitcast_fusion.7
  388.8 2.6 copy.71
  391.4 46.4 %all-to-all-done.6 = f32[8,36,8,256]{3,2,1,0:T(8,128)S(1)} async-done(((f32[8,36,8,256]{3,2,1,0:T(8,128)}), f32[8,36,8,256]{3,2,1,0:T(8,128)S(1)}, u32[]{:S(2)}, u32[]{:S(2)}) %all-to-all-start.6) | async-done | bytes 2359328 | tf_op jit(solution)/shard_map/all_to_all | solution.py:99
  437.7 1.4 copy-done.5
  439.1 6.7 %all-to-all-start.7 = ((f32[8,32,8,256]{3,2,1,0:T(8,128)}), f32[8,32,8,256]{3,2,1,0:T(8,128)}, u32[]{:S(2)}, u32[]{:S(2)}) async-start(f32[8,32,8,256]{3,2,1,0:T(8,128)} %bitcast.304), calls=%async_computation.7 | async-start | bytes 4194304 | tf_op jit(solution)/shard_map/all_to_all | solution.py:99
  445.9 2.6 convolution_bitcast_fusion.11
  448.7 1.3 copy-done.9
  451.1 1.6 copy.125
  455.9 1.7 fusion.30
  458.3 2.0 fusion.36
  460.3 1.4 pad_maximum_fusion.5
  461.7 1.9 collective-permute-start.7
  463.7 1.7 collective-permute-start.8
  467.0 1.6 copy.124
  471.4 19.8 %all-to-all-done.7 = f32[8,32,8,256]{3,2,1,0:T(8,128)} async-done(((f32[8,32,8,256]{3,2,1,0:T(8,128)}), f32[8,32,8,256]{3,2,1,0:T(8,128)}, u32[]{:S(2)}, u32[]{:S(2)}) %all-to-all-start.7) | async-done | bytes 2097184 | tf_op jit(solution)/shard_map/all_to_all | solution.py:99
  491.2 2.6 convolution_bitcast_fusion.6
  494.1 1.3 copy-done.2
  496.0 6.9 %last_product.1 = f32[32,256,256]{2,1,0:T(8,128)} custom-call(f32[32,64,256]{2,1,0:T(8,128)S(1)} %bitcast.298, f32[32,64,256]{2,1,0:T(8,128)S(1)} %bitcast.299, f32[32,64,256]{2,1,0:T(8,128)S(1)} %bitcast.300, f32[32,64,256]{2,1,0:T(8,128)S(1)} %bitcast.301, f32[256,256]{1,0:T(8,128)S(1)} %copy-done.1), custom_call_target="tpu_custom_call" | custom-call | tf_op jit(solution)/shard_map/last_product/pallas_call | solution.py:75
  (112 shorter events, 28.0 us)
Async XLA Ops:
  0.6 19.5 %copy-start = (f32[256,256]{1,0:T(8,128)S(1)}, f32[256,256]{1,0:T(8,128)}, u32[]{:S(2)}) copy-start(f32[256,256]{1,0:T(8,128)} %param.13) | copy-start | bytes 786436
  0.6 7.9 %copy-start.1 = (f32[256,256]{1,0:T(8,128)S(1)}, f32[256,256]{1,0:T(8,128)}, u32[]{:S(2)}) copy-start(f32[256,256]{1,0:T(8,128)} %refs_4_.1) | copy-start | bytes 786436
  8.5 3.4 copy-start.4
  13.5 6.7 %copy-start.7 = (f32[256,256]{1,0:T(8,128)S(1)}, f32[256,256]{1,0:T(8,128)}, u32[]{:S(2)}) copy-start(f32[256,256]{1,0:T(8,128)} %param.15) | copy-start | bytes 786436
  13.5 6.7 %copy-start.17 = (f32[256]{0:T(256)S(1)}, f32[256]{0:T(256)}, u32[]{:S(2)}) copy-start(f32[256]{0:T(256)} %param.17) | copy-start | bytes 3076
  13.5 6.7 %copy-start.18 = (f32[256]{0:T(256)S(1)}, f32[256]{0:T(256)}, u32[]{:S(2)}) copy-start(f32[256]{0:T(256)} %param.16) | copy-start | bytes 3076
  13.5 75.1 %all-to-all-start = ((f32[8,32,8,256]{3,2,1,0:T(8,128)}), f32[8,32,8,256]{3,2,1,0:T(8,128)}, u32[]{:S(2)}, u32[]{:S(2)}) async-start(f32[8,32,8,256]{3,2,1,0:T(8,128)} %bitcast.296), calls=%async_computation | async-start | bytes 4194304 | tf_op jit(solution)/shard_map/all_to_all | solution.py:99
  28.2 4.0 copy-start.20
  88.6 6.1 %copy-start.19 = (f32[4]{0:T(128)S(1)}, f32[4]{0:T(128)}, u32[]{:S(2)}) copy-start(f32[4]{0:T(128)} %param.12) | copy-start | bytes 52
  88.6 62.6 %all-to-all-start.1 = ((f32[8,40,8,256]{3,2,1,0:T(8,128)}), f32[8,40,8,256]{3,2,1,0:T(8,128)S(1)}, u32[]{:S(2)}, u32[]{:S(2)}) async-start(f32[8,40,8,256]{3,2,1,0:T(8,128)} %pad_maximum_fusion), calls=%async_computation.1 | async-start | bytes 5242880 | tf_op jit(solution)/shard_map/all_to_all | solution.py:99
  151.9 7.5 %collective-permute-start = (f32[32,256]{1,0:T(8,128)S(1)}, f32[32,256]{1,0:T(8,128)S(1)}, u32[]{:S(2)}, u32[]{:S(2)}) collective-permute-start(f32[32,256]{1,0:T(8,128)S(1)} %slice.124), channel_id=1, source_target_pairs={{8,0},{16,8},{24,16},{0,24},{9,1},{17,9},{25,17},{1,25},{10,2},{18... | collective-permute-start | bytes 98312 | tf_op jit(solution)/shard_map/ppermute | solution.py:89
  161.1 58.0 %all-to-all-start.2 = ((f32[8,36,8,256]{3,2,1,0:T(8,128)}), f32[8,36,8,256]{3,2,1,0:T(8,128)}, u32[]{:S(2)}, u32[]{:S(2)}) async-start(f32[8,36,8,256]{3,2,1,0:T(8,128)} %pad_maximum_fusion.1), calls=%async_computation.2 | async-start | bytes 4718592 | tf_op jit(solution)/shard_map/all_to_all | solution.py:99
  222.0 52.2 %all-to-all-start.3 = ((f32[8,32,8,256]{3,2,1,0:T(8,128)}), f32[8,32,8,256]{3,2,1,0:T(8,128)}, u32[]{:S(2)}, u32[]{:S(2)}) async-start(f32[8,32,8,256]{3,2,1,0:T(8,128)} %bitcast.303), calls=%async_computation.3 | async-start | bytes 4194304 | tf_op jit(solution)/shard_map/all_to_all | solution.py:99
  228.8 3.8 copy-start.15
  233.6 12.0 %copy-start.21 = (f32[256]{0:T(256)S(1)}, f32[256]{0:T(256)}, u32[]{:S(2)}) copy-start(f32[256]{0:T(256)} %param.18) | copy-start | bytes 3076
  235.0 3.4 collective-permute-start.1
  235.0 3.6 collective-permute-start.2
  236.5 2.8 collective-permute-start.3
  238.1 6.2 %collective-permute-start.4 = (f32[256,256]{0,1:T(8,128)S(1)}, f32[256,256]{0,1:T(8,128)S(1)}, u32[]{:S(2)}, u32[]{:S(2)}) collective-permute-start(f32[256,256]{0,1:T(8,128)S(1)} %get-tuple-element.53), channel_id=1, source_target_pairs={{24,0},{0,8},{8,16},{16,24},{25,1},{1,9},{9,17},{17,25},{26,2},{2,... | collective-permute-start | bytes 786440 | tf_op jit(solution)/shard_map/ppermute | solution.py:89
  250.6 1.4 copy-start.11
  274.2 52.1 %all-to-all-start.4 = ((f32[8,32,8,256]{3,2,1,0:T(8,128)}), f32[8,32,8,256]{3,2,1,0:T(8,128)}, u32[]{:S(2)}, u32[]{:S(2)}) async-start(f32[8,32,8,256]{3,2,1,0:T(8,128)} %bitcast.306), calls=%async_computation.4 | async-start | bytes 4194304 | tf_op jit(solution)/shard_map/all_to_all | solution.py:99
  284.6 1.4 copy-start.13
  326.3 52.4 %all-to-all-start.5 = ((f32[8,32,8,256]{3,2,1,0:T(8,128)}), f32[8,32,8,256]{3,2,1,0:T(8,128)S(1)}, u32[]{:S(2)}, u32[]{:S(2)}) async-start(f32[8,32,8,256]{3,2,1,0:T(8,128)} %bitcast.305), calls=%async_computation.5 | async-start | bytes 4194304 | tf_op jit(solution)/shard_map/all_to_all | solution.py:99
  332.7 2.2 copy-start.14
  334.9 1.6 copy-start.12
  347.2 1.4 copy-start.10
  349.8 3.5 collective-permute-start.5
  378.7 1.4 copy-start.8
  380.1 57.7 %all-to-all-start.6 = ((f32[8,36,8,256]{3,2,1,0:T(8,128)}), f32[8,36,8,256]{3,2,1,0:T(8,128)S(1)}, u32[]{:S(2)}, u32[]{:S(2)}) async-start(f32[8,36,8,256]{3,2,1,0:T(8,128)} %pad_maximum_fusion.2), calls=%async_computation.6 | async-start | bytes 4718592 | tf_op jit(solution)/shard_map/all_to_all | solution.py:99
  437.7 1.4 copy-start.5
  439.1 52.0 %all-to-all-start.7 = ((f32[8,32,8,256]{3,2,1,0:T(8,128)}), f32[8,32,8,256]{3,2,1,0:T(8,128)}, u32[]{:S(2)}, u32[]{:S(2)}) async-start(f32[8,32,8,256]{3,2,1,0:T(8,128)} %bitcast.304), calls=%async_computation.7 | async-start | bytes 4194304 | tf_op jit(solution)/shard_map/all_to_all | solution.py:99
  448.5 1.6 copy-start.9
  455.6 9.8 %copy-start.6 = (f32[8,36,8,256]{3,2,1,0:T(8,128)S(1)}, f32[8,36,8,256]{3,2,1,0:T(8,128)}, u32[]{:S(2)}) copy-start(f32[8,36,8,256]{3,2,1,0:T(8,128)} %copy-done.5) | copy-start | bytes 7077892
  461.7 6.9 %collective-permute-start.6 = (f32[2,128]{1,0:T(2,128)S(1)}, f32[2,128]{1,0:T(2,128)S(1)}, u32[]{:S(2)}, u32[]{:S(2)}) collective-permute-start(f32[2,128]{1,0:T(2,128)S(1)} %broadcast_in_dim.36), channel_id=1, source_target_pairs={{24,0},{0,8},{8,16},{16,24},{25,1},{1,9},{9,17},{17,25},{26,2},{2,... | collective-permute-start | bytes 3080 | tf_op jit(solution)/shard_map/ppermute | solution.py:89
  461.7 6.9 %collective-permute-start.7 = (f32[2,128]{1,0:T(2,128)S(1)}, f32[2,128]{1,0:T(2,128)S(1)}, u32[]{:S(2)}, u32[]{:S(2)}) collective-permute-start(f32[2,128]{1,0:T(2,128)S(1)} %broadcast_in_dim.36), channel_id=1, source_target_pairs={{16,0},{24,8},{0,16},{8,24},{17,1},{25,9},{1,17},{9,25},{18,2},{26... | collective-permute-start | bytes 3080 | tf_op jit(solution)/shard_map/ppermute | solution.py:89
  463.7 4.9 collective-permute-start.8
  467.0 3.5 copy-start.16
  493.8 1.6 copy-start.2
  493.8 2.2 copy-start.3
where the time goes:
time: 512 us; the launch traced here: 503 us
  waiting for transfers between devices  247 us (48%)
  matrix products  88.4 us (17%)
  starting transfers between devices  61.3 us (12%)
  Pallas kernels  55.1 us (11%)
  local copies, waits for them, and re-layouts  36.3 us (7%)
  other arithmetic  9.54 us (2%)
  between operations  5.51 us (1%)
    all_to_all x8, waiting for transfers between devices, exchange(): lax.all_to_all(blocks, 'slab', split_axis=0, concat_axis=0, tiled=True)  244 us
    all_to_all x8, starting transfers between devices, exchange(): lax.all_to_all(blocks, 'slab', split_axis=0, concat_axis=0, tiled=True)  51.7 us
    pallas_call x1, Pallas kernels, partial_edges(): pl.pallas_call(edge_kernel, out_shape=jax.ShapeDtypeStruct((width, 2 * wi...  48.2 us
    dot_general x4, matrix products, outward(): jnp.einsum('xyk,yj->xjk', part, basis_y[:, c * piece:(c + 1) * piece], pr...  20.8 us
    dot_general x4, matrix products, modal(): hat = jnp.einsum('xjk,xi->ijk', lines[c], basis_x, precision=MID)  17 us
    unnamed x45, local copies, waits for them, and re-layouts  11.8 us
  transfers between devices with their start and end apart: 17, of which 10 were waited for; matrix products, arithmetic and copies ran while one was open for 20% of the time, Pallas kernels for 10%

commit v1 on v0

v1 whole, which is shorter than its diff:
```python
import functools

import jax
import jax.numpy as jnp
from jax import lax
from jax.experimental import pallas as pl
from jax.experimental.pallas import tpu as pltpu
from jax.sharding import PartitionSpec as P

ITERS = 2
GROUP = 4
TILE = 8
LANES = 128

HI = lax.Precision.HIGHEST
F32 = jnp.float32
BF16 = jnp.bfloat16
MESH = pl.DeviceIdType.MESH


def split(value):
    top = value.astype(BF16)
    return top, (value - top.astype(F32)).astype(BF16)


def as_left(value):
    top, low = split(value)
    return jnp.concatenate([top, top, low], axis=1)


def as_right(value):
    top, low = split(value)
    return jnp.concatenate([top, low, top], axis=0)


def dot(left, right):
    return jnp.dot(left, right, preferred_element_type=F32)


def exact(left, right):
    return jnp.dot(left, right, preferred_element_type=F32, precision=HI)


def feti_kernel(
    subs, slabs, rows, width,
    source, coarse, rho, basis_x, basis_y, basis_z, eigen_x, eigen_y, eigen_z, stiff,
    fields, own_mult, own_jump,
    source_in, coarse_in, sent, lines, spread, got,
    z_right, zt_right, yt_left, xt_left, x_left, x_t, y_t, stiff_t,
    pair_eigen, yz_eigen, x_column, z_column, first_column, last_column,
    share_first, share_last, beside, parts_in, gathered, ends_in,
    jump_t, search_t, search_in, mult_t, force, edge, sums_out, sums_in,
    in_sem, own_sem, out_sem, fwd_send, fwd_recv, inv_send, inv_recv,
    part_send, part_recv, all_send, all_recv, side_send, side_recv, sum_send, sum_recv,
):
    me = lax.axis_index("slab")
    sub = lax.axis_index("sub")
    chunks = rows // TILE
    lanes = min(width, LANES)
    halves = width // lanes
    step_rows = TILE * halves
    ahead = lambda m: lax.rem(me + m, slabs)
    behind = lambda m: lax.rem(me + slabs - m, slabs)
    next_sub = lax.rem(sub + 1, subs)
    last_sub = lax.rem(sub + subs - 1, subs)
    own_rho = rho[sub]
    weight = 0.5 * (own_rho + rho[next_sub])

    def remote(src, dst, send, recv, target):
        return pltpu.make_async_remote_copy(
            src_ref=src, dst_ref=dst, send_sem=send, recv_sem=recv, device_id=target, device_id_type=MESH
        )

    def fetch(which, g, slot):
        at = pl.ds(g * GROUP, GROUP)
        return (
            pltpu.make_async_copy(source.at[0, at], source_in.at[slot], in_sem.at[0, slot]),
            pltpu.make_async_copy(coarse.at[which, 0, at], coarse_in.at[slot], in_sem.at[1, slot]),
        )

    def start(copies):
        for copy in copies:
            copy.start()

    start(fetch(1, 0, 0))

    barrier = pltpu.get_barrier_semaphore()
    for m in range(1, slabs):
        pl.semaphore_signal(barrier, inc=1, device_id=(sub, ahead(m)), device_id_type=MESH)
    for m in range(1, subs):
        pl.semaphore_signal(barrier, inc=1, device_id=(lax.rem(sub + m, subs), me), device_id_type=MESH)

    z_right[...] = as_right(basis_z[...])
    y_t[...] = basis_y[...].T
    yt_left[...] = as_left(y_t[...])

    pl.semaphore_wait(barrier, slabs + subs - 2)

    def forward(m, c, first, count):
        at = pl.ds(first * step_rows, count * step_rows)
        d = ahead(m)
        return remote(
            sent.at[d * chunks + c, at], lines.at[c * slabs + me, at],
            fwd_send.at[c, m], fwd_recv.at[c, m], (sub, d),
        )

    def forward_all(c, first, count):
        for m in range(1, slabs):
            forward(m, c, first, count).start()

    def transform(which, store, after):
        steps = rows // GROUP

        def step(g, carry):
            slot = lax.rem(g, 2)

            @pl.when(g + 1 < steps)
            def _():
                start(fetch(which, g + 1, 1 - slot))

            for copy in fetch(which, g, slot):
                copy.wait()
            for r in range(GROUP):
                load = source_in[slot, r] + coarse_in[slot, r]
                part = dot(as_left(load), z_right[...])
                part = dot(yt_left[...], as_right(part))
                for h in range(halves):
                    at = pl.ds(pl.multiple_of((g * GROUP + r) * step_rows + h * TILE, TILE), TILE)
                    store[:, at, :] = part[:, h * lanes : (h + 1) * lanes].reshape(width // TILE, TILE, lanes)
            after(g)
            return carry

        lax.fori_loop(0, steps, step, 0)

    transform(1, sent, lambda g: forward_all(0, g * GROUP, GROUP))
    if chunks > 1:
        forward_all(1, 0, rows)

    keep = lambda c: pltpu.make_async_copy(sent.at[me * chunks + c], lines.at[c * slabs + me], own_sem.at[c])
    for c in range(chunks):
        keep(c).start()

    start(fetch(0, 0, 0))
    square = lambda row: jnp.broadcast_to(row, (width, width))
    down = lambda row: square(row).T
    y_column = down(eigen_y[...])
    pair_eigen[...] = y_column + eigen_x[...]
    yz_eigen[...] = y_column + eigen_z[...]
    x_column[...] = down(eigen_x[...])
    z_column[...] = down(eigen_z[...])
    first_column[...] = down(basis_z[0:1, :])
    last_column[...] = down(basis_z[width - 1 : width, :])
    x_t[...] = basis_x[...].T
    xt_left[...] = as_left(x_t[...])
    x_left[...] = as_left(basis_x[...])
    zt_right[...] = as_right(basis_z[...].T)
    stiff_t[...] = stiff[...].T

    transform(0, spread, lambda g: None)

    def line_of(ref, q, at):
        return jnp.concatenate(
            [ref[q, pl.ds(h * TILE + at, rows, stride=step_rows), :] for h in range(halves)], axis=1
        )

    own_x = as_right(basis_x[pl.ds(pl.multiple_of(me * rows, TILE), rows), :])

    def partial_edges(jg, carry):
        at_j = pl.ds(pl.multiple_of(jg * TILE, TILE), TILE)
        eigen = pair_eigen[at_j, :]
        firsts, lasts = [], []
        for at in range(TILE):
            left = as_right_first(line_of(spread, jg, at))
            hat = lax.dot_general(left, own_x, (((0,), (0,)), ((), ())), preferred_element_type=F32)
            modes = hat / (eigen[at : at + 1, :] + z_column[...])
            firsts.append(jnp.sum(modes * first_column[...], axis=0, keepdims=True))
            lasts.append(jnp.sum(modes * last_column[...], axis=0, keepdims=True))
        share_first[at_j, :] = jnp.concatenate(firsts, axis=0) / own_rho
        share_last[at_j, :] = jnp.concatenate(lasts, axis=0) / own_rho
        return carry

    lax.fori_loop(0, width // TILE, partial_edges, 0)

    aside = remote(share_first, beside, side_send.at[0], side_recv.at[0], (last_sub, me))
    aside.start()
    aside.wait()
    share_last[...] = share_last[...] - beside[...]

    own_at = pl.ds(pl.multiple_of(me * rows, TILE), rows)
    scatter = [
        remote(
            share_last.at[pl.ds(pl.multiple_of(ahead(m) * rows, TILE), rows)], parts_in.at[m],
            part_send.at[m], part_recv.at[m], (sub, ahead(m)),
        )
        for m in range(1, slabs)
    ]
    start(scatter)
    rest = [(c, h * (rows // 2), rows // 2) for c in range(2, chunks) for h in range(2)]
    for piece in rest[:1]:
        forward_all(*piece)
    total = share_last[own_at, :]
    for m in range(1, slabs):
        scatter[m - 1].wait_recv()
        total = total + parts_in[m]
    gathered[0, me] = total

    def gather(it):
        return [
            remote(gathered.at[it, me], gathered.at[it, me], all_send.at[it, m], all_recv.at[it, m], (sub, ahead(m)))
            for m in range(1, slabs)
        ]

    gather_first = gather(0)
    start(gather_first)
    for piece in rest[1:]:
        forward_all(*piece)
    for copy in gather_first:
        copy.wait_recv()

    def face(it):
        apart = gathered[it].reshape(width, width)
        jump = exact(exact(basis_y[...], apart), x_t[...])
        modes = exact(exact(y_t[...], jump), basis_x[...]) * stiff_t[...]
        search = exact(exact(basis_y[...], modes), x_t[...]) * weight
        jump_t[...] = jump
        search_t[it] = search
        both = jnp.sum(jump * search, axis=(0, 1), keepdims=True)
        norm = jnp.sum(search * search, axis=(0, 1), keepdims=True)
        line = lax.broadcasted_iota(jnp.int32, (TILE, LANES), 0)
        sums_out[it] = jnp.where(line == 0, both, norm)

    def sums(it):
        return [
            remote(
                sums_out.at[it], sums_in.at[it, m], sum_send.at[it, m], sum_recv.at[it, m],
                (lax.rem(sub + m, subs), me),
            )
            for m in range(1, subs)
        ]

    def step_length(it, copies):
        total = sums_out[it]
        for m in range(1, subs):
            copies[m - 1].wait_recv()
            total = total + sums_in[it, m]
        return total[0:1, 0:1] / (total[1:2, 0:1] + 1e-06)

    face(0)
    sums_first = sums(0)
    start(sums_first)
    pass_on = remote(search_t.at[0], search_in, side_send.at[1], side_recv.at[1], (next_sub, me))
    pass_on.start()
    alpha = step_length(0, sums_first)
    mult_t[...] = alpha * search_t[0]
    force[1] = exact(exact(y_t[...], -mult_t[...]), basis_x[...]).T
    pass_on.wait_recv()
    force[0] = exact(exact(y_t[...], alpha * search_in[...]), basis_x[...]).T

    edge[...] = jnp.zeros_like(edge)

    def modal(c):
        def one(at, carry):
            mine = c * TILE + at
            j = me * rows + mine
            line = jnp.concatenate([line_of(lines, c * slabs + d, at) for d in range(slabs)], axis=0)
            hat = dot(xt_left[...], as_right(line))
            lane = lax.broadcasted_iota(jnp.int32, (width, width), 1)
            pick = lambda p: jnp.sum(jnp.where(lane == j, force[p], 0.0), axis=1, keepdims=True)
            hat = hat + pick(0) * basis_z[0:1, :] + pick(1) * basis_z[width - 1 : width, :]
            modes = hat / ((x_column[...] + yz_eigen[pl.ds(j, 1), :]) * own_rho)
            back = dot(x_left[...], as_right(modes))
            for h in range(halves):
                at_x = pl.ds(pl.multiple_of((h * TILE + at) * rows, TILE), rows)
                part = back[:, h * lanes : (h + 1) * lanes]
                spread[pl.ds(c * slabs, slabs), at_x, :] = part.reshape(slabs, rows, lanes)
            lane = lax.broadcasted_iota(jnp.int32, (width, LANES), 1)
            first = jnp.sum(modes * basis_z[0:1, :], axis=1, keepdims=True)
            last = jnp.sum(modes * basis_z[width - 1 : width, :], axis=1, keepdims=True)
            edge[...] += jnp.where(lane == mine, first, 0.0) + jnp.where(lane == rows + mine, last, 0.0)
            return carry

        for m in range(1, slabs):
            d = behind(m)
            remote(
                sent.at[d * chunks + c], lines.at[c * slabs + d], fwd_send.at[c, m], fwd_recv.at[c, m], (sub, d)
            ).wait_recv()
        keep(c).wait()
        lax.fori_loop(0, TILE, one, 0)

    def inverse(c):
        return [
            remote(
                spread.at[c * slabs + ahead(m)], got.at[c * slabs + me],
                inv_send.at[c, m], inv_recv.at[c, m], (sub, ahead(m)),
            )
            for m in range(1, slabs)
        ]

    back = [inverse(c) for c in range(chunks)]
    stay = lambda c: pltpu.make_async_copy(spread.at[c * slabs + me], got.at[c * slabs + me], own_sem.at[c])
    early = max(chunks // 2, 1)
    for c in range(chunks):
        modal(c)
        stay(c).start()
        if c < early:
            start(back[c])

    edge_t = edge[...].T
    ends_in[0] = edge_t[:rows]
    send_ends = remote(ends_in.at[0], ends_in.at[1], side_send.at[2], side_recv.at[2], (last_sub, me))
    send_ends.start()
    send_ends.wait_recv()
    gathered[1, me] = edge_t[rows : 2 * rows] - ends_in[1]
    gather_last = gather(1)
    start(gather_last)
    for c in range(early, chunks):
        start(back[c])

    write = lambda c: pltpu.make_async_copy(
        got.at[pl.ds(c * slabs, slabs)], fields.at[pl.ds(c * slabs, slabs)], out_sem.at[c]
    )

    def arrive(c):
        stay(c).wait()
        for m in range(1, slabs):
            d = behind(m)
            remote(
                spread.at[c * slabs + d], got.at[c * slabs + d], inv_send.at[c, m], inv_recv.at[c, m], (sub, d)
            ).wait_recv()

        def one(d, carry):
            at = [pl.ds(h * TILE * rows, TILE * rows) for h in range(halves)]
            whole = jnp.concatenate([got[c * slabs + d, at[h], :] for h in range(halves)], axis=1)
            whole = dot(as_left(whole), zt_right[...])
            for h in range(halves):
                got[c * slabs + d, at[h], :] = whole[:, h * lanes : (h + 1) * lanes]
            return carry

        lax.fori_loop(0, slabs, one, 0)
        write(c).start()

    for c in range(early):
        arrive(c)

    for copy in gather_last:
        copy.wait_recv()
    face(1)
    sums_last = sums(1)
    start(sums_last)
    alpha = step_length(1, sums_last)
    mult_t[...] = (mult_t[...] + alpha * search_t[1]).T
    own_mult[...] = mult_t[own_at, :]
    jump_t[...] = jump_t[...].T
    own_jump[...] = jump_t[own_at, :]

    for copies in (scatter, gather_first, gather_last, sums_first, sums_last, [pass_on, send_ends]):
        for copy in copies:
            copy.wait_send()
    for c in range(chunks):
        for m in range(1, slabs):
            forward(m, c, 0, rows).wait_send()

    for c in range(early, chunks):
        arrive(c)
    for c in range(chunks):
        write(c).wait()
        for copy in back[c]:
            copy.wait_send()


def as_right_first(value):
    top, low = split(value)
    return jnp.concatenate([top, top, low], axis=0)


def iterate(subs, slabs, source, coarse, rho, basis_x, basis_y, basis_z, eigen_x, eigen_y, eigen_z, stiff):
    rows, width = source.shape[1:3]
    chunks = rows // TILE
    face = lambda *lead: pltpu.VMEM((*lead, width, width), F32)
    lot = lambda *lead: pltpu.VMEM((*lead, rows, width), F32)
    lanes = min(width, LANES)
    block = (chunks * slabs, TILE * rows * (width // lanes), lanes)
    field = lambda: pltpu.VMEM(block, F32)
    dma = pltpu.SemaphoreType.DMA
    vmem = pl.BlockSpec(memory_space=pltpu.VMEM)
    hbm = pl.BlockSpec(memory_space=pl.ANY)
    return pl.pallas_call(
        functools.partial(feti_kernel, subs, slabs, rows, width),
        out_shape=(
            jax.ShapeDtypeStruct(block, F32),
            jax.ShapeDtypeStruct((rows, width), F32),
            jax.ShapeDtypeStruct((rows, width), F32),
        ),
        in_specs=[hbm, hbm, pl.BlockSpec(memory_space=pltpu.SMEM)] + [vmem] * 7,
        out_specs=(hbm, vmem, vmem),
        scratch_shapes=[
            face(2, GROUP), face(2, GROUP), field(), field(), field(), field(),
            pltpu.VMEM((3 * width, width), BF16), pltpu.VMEM((3 * width, width), BF16),
            pltpu.VMEM((width, 3 * width), BF16), pltpu.VMEM((width, 3 * width), BF16),
            pltpu.VMEM((width, 3 * width), BF16), face(), face(), face(),
            face(), face(), face(), face(), face(), face(),
            face(), face(), face(), lot(slabs), lot(ITERS, slabs), lot(2),
            face(), face(ITERS), face(), face(), face(2), pltpu.VMEM((width, LANES), F32),
            pltpu.VMEM((ITERS, TILE, LANES), F32), pltpu.VMEM((ITERS, subs, TILE, LANES), F32),
            dma((2, 2)), dma((chunks,)), dma((chunks,)),
            dma((chunks, slabs)), dma((chunks, slabs)), dma((chunks, slabs)), dma((chunks, slabs)),
            dma((slabs,)), dma((slabs,)), dma((ITERS, slabs)), dma((ITERS, slabs)),
            dma((3,)), dma((3,)), dma((ITERS, subs)), dma((ITERS, subs)),
        ],
        compiler_params=pltpu.CompilerParams(
            collective_id=0, has_side_effects=True, vmem_limit_bytes=60 * 2**20
        ),
        name="feti",
    )(source, coarse, rho, basis_x, basis_y, basis_z, eigen_x, eigen_y, eigen_z, stiff)


def last_kernel(field_ref, basis_ref, out_ref):
    left = as_left(basis_ref[...])
    blocks, halves, lot, count, lanes = field_ref.shape
    for at in range(count):
        parts = [field_ref[:, h, :, at, :].reshape(blocks * lot, lanes) for h in range(halves)]
        out_ref[at] = dot(left, as_right(jnp.concatenate(parts, axis=1)))


def last_product(fields, basis_y):
    blocks, halves, lot, rows, lanes = fields.shape
    width = basis_y.shape[0]
    return pl.pallas_call(
        last_kernel,
        out_shape=jax.ShapeDtypeStruct((rows, width, halves * lanes), F32),
        grid=(rows // TILE,),
        in_specs=[
            pl.BlockSpec((blocks, halves, lot, TILE, lanes), lambda x: (0, 0, 0, x, 0)),
            pl.BlockSpec((width, width), lambda x: (0, 0)),
        ],
        out_specs=pl.BlockSpec((TILE, width, halves * lanes), lambda x: (x, 0, 0)),
        compiler_params=pltpu.CompilerParams(vmem_limit_bytes=24 * 2**20),
        name="last_product",
    )(fields, basis_y)


def on_device(
    source, coarse, rho, basis_x, basis_y, basis_z, eigen_x, eigen_y, eigen_z, face_stiff
):
    subs = lax.axis_size("sub")
    slabs = lax.axis_size("slab")
    rows, width = source.shape[1:3]
    fields, multipliers, jump = iterate(
        subs, slabs, source, coarse, rho, basis_x, basis_y, basis_z,
        eigen_x[None], eigen_y[None], eigen_z[None], face_stiff,
    )
    chunks = rows // TILE
    turned = basis_y.reshape(width, slabs, chunks, TILE).swapaxes(1, 2).reshape(width, width)
    lanes = min(width, LANES)
    fields = fields.reshape(chunks * slabs, width // lanes, TILE, rows, lanes)
    solution = last_product(fields, turned)
    return (solution[None], multipliers[None], jump[None])


def solution(mesh):
    in_specs = (
        P("sub", "slab", None, None),
        P(None, "sub", "slab", None, None),
        P(),
        P(),
        P(),
        P(),
        P(),
        P(),
        P(),
        P(),
    )
    out_specs = (P("sub", "slab", None, None), P("sub", "slab", None), P("sub", "slab", None))
    return jax.shard_map(
        on_device, mesh=mesh, in_specs=in_specs, out_specs=out_specs, check_vma=False
    )
```

time: 512 us -> 409 us (0.80)
  Pallas kernels: 55.1 us -> 397 us
  waiting for transfers between devices: 247 us -> 0 us
  matrix products: 88.4 us -> 0 us
  starting transfers between devices: 61.3 us -> 0 us
  local copies, waits for them, and re-layouts: 36.3 us -> 5.84 us
  other arithmetic: 9.54 us -> 0 us
    pallas_call x1, Pallas kernels: 48.2 us -> 388 us  [iterate(): pl.pallas_call(functools.partial(feti_kernel, subs, slabs, rows, width),...]
    all_to_all x8 -> x0, waiting for transfers between devices: 244 us -> none  [exchange(): lax.all_to_all(blocks, 'slab', split_axis=0, concat_axis=0, tiled=True)]
    dot_general x37 -> x0, matrix products: 88.4 us -> none  [the longest x4 20.8 us: outward(): jnp.einsum('xyk,yj->xjk', part, basis_y[:, c * piece:(c + 1) * piece], pr...]
    all_to_all x8 -> x0, starting transfers between devices: 51.7 us -> none  [exchange(): lax.all_to_all(blocks, 'slab', split_axis=0, concat_axis=0, tiled=True)]
    dot_general x5 -> x0, local copies, waits for them, and re-layouts: 9.73 us -> none  [the longest x4 8.87 us: modal(): spread = jnp.einsum('ijk,xi->xjk', modes, basis_x, precision=MID)]
    ppermute x9 -> x0, starting transfers between devices: 9.59 us -> none  [from_behind(): lax.ppermute(block, axis, [((i - distance) % count, i) for i in range(cou...]
    unnamed x45 -> x9, local copies, waits for them, and re-layouts: 11.8 us -> 5.69 us
  transfers between devices with their start and end apart: 17 -> 0, of which waited for: 10 -> 0; matrix products, arithmetic and copies ran while one was open for 20% -> 0% of each run, Pallas kernels for 10% -> 0%
where the time goes in v1:
time: 409 us; the launch traced here: 404 us
  Pallas kernels  397 us (97%)
  local copies, waits for them, and re-layouts  5.84 us (1%)
    pallas_call x1, Pallas kernels, iterate(): pl.pallas_call(functools.partial(feti_kernel, subs, slabs, rows, width),...  388 us
    pallas_call x1, Pallas kernels, last_product(): pl.pallas_call(last_kernel, out_shape=jax.ShapeDtypeStruct((rows, width,...  9.71 us

profile of v1, /device:TPU:8, one launch (start us, length us, event | category | flops | bytes accessed | tf_op | source)
XLA Modules:
  0.0 403.9 jit_solution(88153914149702615)
XLA Ops:
  0.6 1.1 copy.14
  1.7 0.1 copy.16.basis_ref
  1.9 387.7 %feti.1 = (f32[32,512,128]{2,1,0:T(8,128)}, f32[32,256]{1,0:T(8,128)}, f32[32,256]{1,0:T(8,128)}) custom-call(f32[1,32,256,256]{3,2,1,0:T(8,128)} %source.1, f32[2,1,32,256,256]{4,3,2,1,0:T(8,128)} %coarse.1, f32[4]{0:T(128)} %rho.1, f32[256,256]{1,0:T(8,128)} %basis_x.1, f32[256,256]{1,0:T(8,128)} %basis_y.1, f32[256,256]{1,0:T(8,128)} %basis_z.1, ...), custom_call_target="tpu_custom_call" | custom-call | tf_op jit(solution)/shard_map/feti/pallas_call | solution.py:387
  389.6 0.0 copy-start
  389.6 3.4 copy-done
  393.0 0.0 copy-start.2
  393.0 0.0 copy-start.1
  393.0 9.7 %last_product.1 = f32[32,256,256]{2,1,0:T(8,128)} custom-call(f32[32,2,8,32,128]{4,3,2,1,0:T(8,128)S(1)} %bitcast.11, f32[256,256]{1,0:T(8,128)S(1)} %copy.16.basis_ref), custom_call_target="tpu_custom_call" | custom-call | tf_op jit(solution)/shard_map/last_product/pallas_call | solution.py:428
  402.7 0.0 copy-done.2
  402.7 0.6 copy.19
  403.3 0.0 copy-done.1
  403.3 0.6 copy.20
  (1 shorter events, 0.0 us)
Async XLA Ops:
  389.6 3.4 copy-start
  393.0 9.7 %copy-start.2 = (f32[32,256]{1,0:T(8,128)S(1)}, f32[32,256]{1,0:T(8,128)}, u32[]{:S(2)}) copy-start(f32[32,256]{1,0:T(8,128)} %get-tuple-element.7) | copy-start | bytes 98308
  393.0 10.3 %copy-start.1 = (f32[32,256]{1,0:T(8,128)S(1)}, f32[32,256]{1,0:T(8,128)}, u32[]{:S(2)}) copy-start(f32[32,256]{1,0:T(8,128)} %get-tuple-element.8) | copy-start | bytes 98308

commit v2 on v1

--- a/solution.py
+++ b/solution.py
@@ -44,14 +44,14 @@
 def feti_kernel(
     subs, slabs, rows, width,
     source, coarse, rho, basis_x, basis_y, basis_z, eigen_x, eigen_y, eigen_z, stiff,
-    fields, own_mult, own_jump,
+    solved, own_mult, own_jump,
     source_in, coarse_in, sent, lines, spread, got,
     z_right, zt_right, yt_left, xt_left, x_left, x_t, y_t, stiff_t,
     pair_eigen, yz_eigen, x_column, z_column, first_column, last_column,
-    share_first, share_last, beside, parts_in, gathered, ends_in,
+    y_parts, share_first, share_last, beside, parts_in, half_sum, gathered, gathered_last, ends_in,
     jump_t, search_t, search_in, mult_t, force, edge, sums_out, sums_in,
-    in_sem, own_sem, out_sem, fwd_send, fwd_recv, inv_send, inv_recv,
-    part_send, part_recv, all_send, all_recv, side_send, side_recv, sum_send, sum_recv,
+    in_sem, own_sem, fwd_send, fwd_recv, inv_send, inv_recv, last_send, last_recv,
+    part_send, part_recv, mirror_send, mirror_recv, all_send, all_recv, side_send, side_recv, sum_send, sum_recv,
 ):
     me = lax.axis_index("slab")
     sub = lax.axis_index("sub")
@@ -61,6 +61,11 @@
     step_rows = TILE * halves
     ahead = lambda m: lax.rem(me + m, slabs)
     behind = lambda m: lax.rem(me + slabs - m, slabs)
+    half = slabs // 2
+    block = lax.rem(me, half)
+    side = me - block
+    mirror = lax.rem(me + half, slabs)
+    peer = lambda m: lax.rem(block + m, half)
     next_sub = lax.rem(sub + 1, subs)
     last_sub = lax.rem(sub + subs - 1, subs)
     own_rho = rho[sub]
@@ -155,8 +160,15 @@
     x_left[...] = as_left(basis_x[...])
     zt_right[...] = as_right(basis_z[...].T)
     stiff_t[...] = stiff[...].T
+    for c in range(chunks):
+        own_y = jnp.concatenate([y_t[d * rows + c * TILE : d * rows + (c + 1) * TILE, :] for d in range(slabs)], axis=0)
+        y_parts[c] = padded(own_y, True).T.astype(BF16)
 
     transform(0, spread, lambda g: None)
+    quarter = rows // 4
+    rest = [(c, q * quarter, quarter) for c in range(2, chunks) for q in range(4)]
+    for piece in rest[:1]:
+        forward_all(*piece)
 
     def line_of(ref, q, at):
         return jnp.concatenate(
@@ -187,38 +199,40 @@
     share_last[...] = share_last[...] - beside[...]
 
     own_at = pl.ds(pl.multiple_of(me * rows, TILE), rows)
+    lot = width // half
+    lot_at = lambda b: pl.ds(pl.multiple_of(b * lot, TILE), lot)
     scatter = [
-        remote(
-            share_last.at[pl.ds(pl.multiple_of(ahead(m) * rows, TILE), rows)], parts_in.at[m],
-            part_send.at[m], part_recv.at[m], (sub, ahead(m)),
-        )
-        for m in range(1, slabs)
+        remote(share_last.at[lot_at(peer(m))], parts_in.at[m], part_send.at[m], part_recv.at[m], (sub, side + peer(m)))
+        for m in range(1, half)
     ]
     start(scatter)
-    rest = [(c, h * (rows // 2), rows // 2) for c in range(2, chunks) for h in range(2)]
-    for piece in rest[:1]:
+    for piece in rest[1:2]:
         forward_all(*piece)
-    total = share_last[own_at, :]
-    for m in range(1, slabs):
+    total = share_last[lot_at(block), :]
+    for m in range(1, half):
         scatter[m - 1].wait_recv()
         total = total + parts_in[m]
-    gathered[0, me] = total
-
-    def gather(it):
-        return [
-            remote(gathered.at[it, me], gathered.at[it, me], all_send.at[it, m], all_recv.at[it, m], (sub, ahead(m)))
-            for m in range(1, slabs)
-        ]
-
-    gather_first = gather(0)
+    half_sum[...] = total
+    swap = remote(half_sum, parts_in.at[0], mirror_send.at[0], mirror_recv.at[0], (sub, mirror))
+    swap.start()
+    for piece in rest[2:3]:
+        forward_all(*piece)
+    swap.wait_recv()
+    gathered[lot_at(block), :] = total + parts_in[0]
+    gather_first = [
+        remote(
+            gathered.at[lot_at(block)], gathered.at[lot_at(block)], all_send.at[0, m], all_recv.at[0, m],
+            (sub, side + peer(m)),
+        )
+        for m in range(1, half)
+    ]
     start(gather_first)
-    for piece in rest[1:]:
+    for piece in rest[3:]:
         forward_all(*piece)
     for copy in gather_first:
         copy.wait_recv()
 
-    def face(it):
-        apart = gathered[it].reshape(width, width)
+    def face(it, apart):
         jump = exact(exact(basis_y[...], apart), x_t[...])
         modes = exact(exact(y_t[...], jump), basis_x[...]) * stiff_t[...]
         search = exact(exact(basis_y[...], modes), x_t[...]) * weight
@@ -245,7 +259,7 @@
             total = total + sums_in[it, m]
         return total[0:1, 0:1] / (total[1:2, 0:1] + 1e-06)
 
-    face(0)
+    face(0, gathered[...])
     sums_first = sums(0)
     start(sums_first)
     pass_on = remote(search_t.at[0], search_in, side_send.at[1], side_recv.at[1], (next_sub, me))
@@ -269,10 +283,10 @@
             hat = hat + pick(0) * basis_z[0:1, :] + pick(1) * basis_z[width - 1 : width, :]
             modes = hat / ((x_column[...] + yz_eigen[pl.ds(j, 1), :]) * own_rho)
             back = dot(x_left[...], as_right(modes))
-            for h in range(halves):
-                at_x = pl.ds(pl.multiple_of((h * TILE + at) * rows, TILE), rows)
-                part = back[:, h * lanes : (h + 1) * lanes]
-                spread[pl.ds(c * slabs, slabs), at_x, :] = part.reshape(slabs, rows, lanes)
+            for d in range(slabs):
+                for h in range(halves):
+                    at_x = pl.ds(h * TILE + at, rows, stride=step_rows)
+                    spread[c * slabs + d, at_x, :] = back[d * rows : (d + 1) * rows, h * lanes : (h + 1) * lanes]
             lane = lax.broadcasted_iota(jnp.int32, (width, LANES), 1)
             first = jnp.sum(modes * basis_z[0:1, :], axis=1, keepdims=True)
             last = jnp.sum(modes * basis_z[width - 1 : width, :], axis=1, keepdims=True)
@@ -287,64 +301,115 @@
         keep(c).wait()
         lax.fori_loop(0, TILE, one, 0)
 
-    def inverse(c):
-        return [
-            remote(
-                spread.at[c * slabs + ahead(m)], got.at[c * slabs + me],
-                inv_send.at[c, m], inv_recv.at[c, m], (sub, ahead(m)),
-            )
-            for m in range(1, slabs)
-        ]
-
-    back = [inverse(c) for c in range(chunks)]
+    last = chunks - 1
+    quarters = [pl.ds(q * quarter * step_rows, quarter * step_rows) for q in range(4)]
+
+    def inverse(c, m, q=None):
+        d = ahead(m)
+        src, dst = spread.at[c * slabs + d], got.at[c * slabs + me]
+        if q is None:
+            return remote(src, dst, inv_send.at[c, m], inv_recv.at[c, m], (sub, d))
+        return remote(src.at[quarters[q]], dst.at[quarters[q]], last_send.at[q, m], last_recv.at[q, m], (sub, d))
+
+    def inverse_from(c, m, q=None):
+        d = behind(m)
+        src, dst = spread.at[c * slabs + d], got.at[c * slabs + d]
+        if q is None:
+            return remote(src, dst, inv_send.at[c, m], inv_recv.at[c, m], (sub, d))
+        return remote(src.at[quarters[q]], dst.at[quarters[q]], last_send.at[q, m], last_recv.at[q, m], (sub, d))
+
     stay = lambda c: pltpu.make_async_copy(spread.at[c * slabs + me], got.at[c * slabs + me], own_sem.at[c])
-    early = max(chunks // 2, 1)
+    back = []
+
+    def give(c):
+        copies = [inverse(c, m, q) for q in (range(4) if c == last else [None]) for m in range(1, slabs)]
+        start(copies)
+        back.extend(copies)
+
     for c in range(chunks):
         modal(c)
         stay(c).start()
-        if c < early:
-            start(back[c])
+        if c == 0 and last > 0:
+            give(c)
 
     edge_t = edge[...].T
     ends_in[0] = edge_t[:rows]
     send_ends = remote(ends_in.at[0], ends_in.at[1], side_send.at[2], side_recv.at[2], (last_sub, me))
     send_ends.start()
     send_ends.wait_recv()
-    gathered[1, me] = edge_t[rows : 2 * rows] - ends_in[1]
-    gather_last = gather(1)
-    start(gather_last)
-    for c in range(early, chunks):
-        start(back[c])
-
-    write = lambda c: pltpu.make_async_copy(
-        got.at[pl.ds(c * slabs, slabs)], fields.at[pl.ds(c * slabs, slabs)], out_sem.at[c]
+    gathered_last[own_at, :] = edge_t[rows : 2 * rows] - ends_in[1]
+    far_at = pl.ds(pl.multiple_of(mirror * rows, TILE), rows)
+
+    def hand(at, k, m, target):
+        return remote(gathered_last.at[at], gathered_last.at[at], all_send.at[k, m], all_recv.at[k, m], (sub, target))
+
+    swap_last = remote(
+        gathered_last.at[own_at], gathered_last.at[own_at], mirror_send.at[1], mirror_recv.at[1], (sub, mirror)
     )
+    swap_last.start()
+    gather_own = [hand(own_at, 1, m, side + peer(m)) for m in range(1, half)]
+    gather_far = [hand(far_at, 2, m, side + peer(m)) for m in range(1, half)]
+    start(gather_own)
+    for c in range(1, min(2, last)):
+        give(c)
+
+    def finish(c, q):
+        def depth(d, carry):
+            whole = got[c * slabs + d, quarters_at(q), :].reshape(quarter, halves, TILE, lanes)
+            whole = jnp.concatenate([whole[:, h].reshape(quarter * TILE, lanes) for h in range(halves)], axis=1)
+            whole = dot(as_left(whole), zt_right[...])
+            whole = [whole[:, h * lanes : (h + 1) * lanes].reshape(quarter, 1, TILE, lanes) for h in range(halves)]
+            got[c * slabs + d, quarters_at(q), :] = jnp.concatenate(whole, axis=1).reshape(quarter * step_rows, lanes)
+            return carry
+
+        lax.fori_loop(0, slabs, depth, 0)
+
+        def across(r, carry):
+            x = q * quarter + r
+            at = [pl.ds(pl.multiple_of(x * step_rows + h * TILE, TILE), TILE) for h in range(halves)]
+            right = jnp.concatenate(
+                [
+                    jnp.concatenate([got[c * slabs + d, at[h], :] for d in range(slabs)], axis=0)
+                    for h in range(halves)
+                ],
+                axis=1,
+            )
+            part = dot(y_parts[c], padded(right, False).astype(BF16))
+            solved[x] = part if c == 0 else solved[x] + part
+            return carry
+
+        lax.fori_loop(0, quarter, across, 0)
+
+    quarters_at = lambda q: pl.ds(pl.multiple_of(q * quarter * step_rows, TILE), quarter * step_rows)
 
     def arrive(c):
         stay(c).wait()
-        for m in range(1, slabs):
-            d = behind(m)
-            remote(
-                spread.at[c * slabs + d], got.at[c * slabs + d], inv_send.at[c, m], inv_recv.at[c, m], (sub, d)
-            ).wait_recv()
-
-        def one(d, carry):
-            at = [pl.ds(h * TILE * rows, TILE * rows) for h in range(halves)]
-            whole = jnp.concatenate([got[c * slabs + d, at[h], :] for h in range(halves)], axis=1)
-            whole = dot(as_left(whole), zt_right[...])
-            for h in range(halves):
-                got[c * slabs + d, at[h], :] = whole[:, h * lanes : (h + 1) * lanes]
-            return carry
-
-        lax.fori_loop(0, slabs, one, 0)
-        write(c).start()
-
-    for c in range(early):
+        if c < last:
+            for m in range(1, slabs):
+                inverse_from(c, m).wait_recv()
+
+            def one(q, carry):
+                finish(c, q)
+                return carry
+
+            lax.fori_loop(0, 4, one, 0)
+        else:
+            for q in range(4):
+                for m in range(1, slabs):
+                    inverse_from(c, m, q).wait_recv()
+                finish(c, q)
+
+    if last > 0:
+        arrive(0)
+    swap_last.wait_recv()
+    start(gather_far)
+    for c in range(min(2, last), chunks):
+        give(c)
+    for c in range(1, last - 1):
         arrive(c)
-
-    for copy in gather_last:
+    for copy in gather_own + gather_far:
         copy.wait_recv()
-    face(1)
+    face(1, gathered_last[...])
     sums_last = sums(1)
     start(sums_last)
     alpha = step_length(1, sums_last)
@@ -353,19 +418,28 @@
     jump_t[...] = jump_t[...].T
     own_jump[...] = jump_t[own_at, :]
 
-    for copies in (scatter, gather_first, gather_last, sums_first, sums_last, [pass_on, send_ends]):
+    small = [scatter, [swap, swap_last, pass_on, send_ends], gather_first, gather_own, gather_far, sums_first, sums_last]
+    for copies in small:
         for copy in copies:
             copy.wait_send()
     for c in range(chunks):
         for m in range(1, slabs):
             forward(m, c, 0, rows).wait_send()
 
-    for c in range(early, chunks):
+    for c in range(max(1, last - 1) if last else 0, chunks):
         arrive(c)
-    for c in range(chunks):
-        write(c).wait()
-        for copy in back[c]:
-            copy.wait_send()
+    for copy in back:
+        copy.wait_send()
+
+
+def padded(value, left):
+    top = value.astype(BF16).astype(F32)
+    low = value - top
+    parts = [top, top, low] if left else [top, low, top]
+    over = -3 * value.shape[0] % LANES
+    if over:
+        parts.append(jnp.zeros((over, value.shape[1]), F32))
+    return jnp.concatenate(parts, axis=0)
 
 
 def as_right_first(value):
@@ -379,64 +453,44 @@
     face = lambda *lead: pltpu.VMEM((*lead, width, width), F32)
     lot = lambda *lead: pltpu.VMEM((*lead, rows, width), F32)
     lanes = min(width, LANES)
-    block = (chunks * slabs, TILE * rows * (width // lanes), lanes)
-    field = lambda: pltpu.VMEM(block, F32)
+    field = lambda: pltpu.VMEM((chunks * slabs, TILE * rows * (width // lanes), lanes), F32)
+    half = slabs // 2
+    stack = 3 * slabs * TILE
+    stack += -stack % LANES
     dma = pltpu.SemaphoreType.DMA
     vmem = pl.BlockSpec(memory_space=pltpu.VMEM)
     hbm = pl.BlockSpec(memory_space=pl.ANY)
     return pl.pallas_call(
         functools.partial(feti_kernel, subs, slabs, rows, width),
         out_shape=(
-            jax.ShapeDtypeStruct(block, F32),
-            jax.ShapeDtypeStruct((rows, width), F32),
-            jax.ShapeDtypeStruct((rows, width), F32),
+            pltpu.VMEM((rows, width, width), F32),
+            pltpu.VMEM((rows, width), F32),
+            pltpu.VMEM((rows, width), F32),
         ),
         in_specs=[hbm, hbm, pl.BlockSpec(memory_space=pltpu.SMEM)] + [vmem] * 7,
-        out_specs=(hbm, vmem, vmem),
+        out_specs=(vmem, vmem, vmem),
         scratch_shapes=[
             face(2, GROUP), face(2, GROUP), field(), field(), field(), field(),
             pltpu.VMEM((3 * width, width), BF16), pltpu.VMEM((3 * width, width), BF16),
             pltpu.VMEM((width, 3 * width), BF16), pltpu.VMEM((width, 3 * width), BF16),
             pltpu.VMEM((width, 3 * width), BF16), face(), face(), face(),
             face(), face(), face(), face(), face(), face(),
-            face(), face(), face(), lot(slabs), lot(ITERS, slabs), lot(2),
+            pltpu.VMEM((chunks, width, stack), BF16),
+            face(), face(), face(), pltpu.VMEM((half, width // half, width), F32),
+            pltpu.VMEM((width // half, width), F32), face(), face(), lot(2),
             face(), face(ITERS), face(), face(), face(2), pltpu.VMEM((width, LANES), F32),
             pltpu.VMEM((ITERS, TILE, LANES), F32), pltpu.VMEM((ITERS, subs, TILE, LANES), F32),
-            dma((2, 2)), dma((chunks,)), dma((chunks,)),
+            dma((2, 2)), dma((chunks,)),
             dma((chunks, slabs)), dma((chunks, slabs)), dma((chunks, slabs)), dma((chunks, slabs)),
-            dma((slabs,)), dma((slabs,)), dma((ITERS, slabs)), dma((ITERS, slabs)),
+            dma((4, slabs)), dma((4, slabs)),
+            dma((half,)), dma((half,)), dma((2,)), dma((2,)), dma((3, half)), dma((3, half)),
             dma((3,)), dma((3,)), dma((ITERS, subs)), dma((ITERS, subs)),
         ],
         compiler_params=pltpu.CompilerParams(
-            collective_id=0, has_side_effects=True, vmem_limit_bytes=60 * 2**20
+            collective_id=0, has_side_effects=True, vmem_limit_bytes=54 * 2**20
         ),
         name="feti",
     )(source, coarse, rho, basis_x, basis_y, basis_z, eigen_x, eigen_y, eigen_z, stiff)
-
-
-def last_kernel(field_ref, basis_ref, out_ref):
-    left = as_left(basis_ref[...])
-    blocks, halves, lot, count, lanes = field_ref.shape
-    for at in range(count):
-        parts = [field_ref[:, h, :, at, :].reshape(blocks * lot, lanes) for h in range(halves)]
-        out_ref[at] = dot(left, as_right(jnp.concatenate(parts, axis=1)))
-
-
-def last_product(fields, basis_y):
-    blocks, halves, lot, rows, lanes = fields.shape
-    width = basis_y.shape[0]
-    return pl.pallas_call(
-        last_kernel,
-        out_shape=jax.ShapeDtypeStruct((rows, width, halves * lanes), F32),
-        grid=(rows // TILE,),
-        in_specs=[
-            pl.BlockSpec((blocks, halves, lot, TILE, lanes), lambda x: (0, 0, 0, x, 0)),
-            pl.BlockSpec((width, width), lambda x: (0, 0)),
-        ],
-        out_specs=pl.BlockSpec((TILE, width, halves * lanes), lambda x: (x, 0, 0)),
-        compiler_params=pltpu.CompilerParams(vmem_limit_bytes=24 * 2**20),
-        name="last_product",
-    )(fields, basis_y)
 
 
 def on_device(
@@ -444,17 +498,11 @@
 ):
     subs = lax.axis_size("sub")
     slabs = lax.axis_size("slab")
-    rows, width = source.shape[1:3]
-    fields, multipliers, jump = iterate(
+    solved, multipliers, jump = iterate(
         subs, slabs, source, coarse, rho, basis_x, basis_y, basis_z,
         eigen_x[None], eigen_y[None], eigen_z[None], face_stiff,
     )
-    chunks = rows // TILE
-    turned = basis_y.reshape(width, slabs, chunks, TILE).swapaxes(1, 2).reshape(width, width)
-    lanes = min(width, LANES)
-    fields = fields.reshape(chunks * slabs, width // lanes, TILE, rows, lanes)
-    solution = last_product(fields, turned)
-    return (solution[None], multipliers[None], jump[None])
+    return (solved[None], multipliers[None], jump[None])
 
 
 def solution(mesh):

time: 409 us -> 383 us (0.936)
  Pallas kernels: 397 us -> 376 us
    pallas_call x1, Pallas kernels: 388 us -> 376 us  [iterate(): pl.pallas_call(functools.partial(feti_kernel, subs, slabs, rows, width),...]
    pallas_call x1 -> x0, Pallas kernels: 9.71 us -> none  [last_product(): pl.pallas_call(last_kernel, out_shape=jax.ShapeDtypeStruct((rows, width,...]
where the time goes in v2:
time: 383 us; the launch traced here: 382 us
  Pallas kernels  376 us (98%)
  local copies, waits for them, and re-layouts  4.63 us (1%)
    pallas_call x1, Pallas kernels, iterate(): pl.pallas_call(functools.partial(feti_kernel, subs, slabs, rows, width),...  376 us

profile of v2, /device:TPU:8, one launch (start us, length us, event | category | flops | bytes accessed | tf_op | source)
XLA Modules:
  0.0 381.6 jit_solution(14500454070166585733)
XLA Ops:
  0.6 376.3 %feti.1 = (f32[32,256,256]{2,1,0:T(8,128)S(1)}, f32[32,256]{1,0:T(8,128)S(1)}, f32[32,256]{1,0:T(8,128)S(1)}) custom-call(f32[1,32,256,256]{3,2,1,0:T(8,128)} %source.1, f32[2,1,32,256,256]{4,3,2,1,0:T(8,128)} %coarse.1, f32[4]{0:T(128)} %rho.1, f32[256,256]{1,0:T(8,128)} %basis_x.1, f32[256,256]{1,0:T(8,128)} %basis_y.1, f32[256,256]{1,0:T(8,128)} %basis_z.1, ...), custom_call_target="tpu_custom_call" | custom-call | tf_op jit(solution)/shard_map/feti/pallas_call | solution.py:463
  377.0 3.4 copy.16
  380.4 0.6 copy.17
  381.0 0.6 copy.18

commit v3 on v2

--- a/solution.py
+++ b/solution.py
@@ -8,7 +8,9 @@
 from jax.sharding import PartitionSpec as P
 
 ITERS = 2
-GROUP = 4
+GROUP = 2
+PIECES = 8
+HAND_OUT = 8
 TILE = 8
 LANES = 128
 
@@ -43,7 +45,16 @@
 
 def feti_kernel(
     subs, slabs, rows, width,
-    source, coarse, rho, basis_x, basis_y, basis_z, eigen_x, eigen_y, eigen_z, stiff,
+    source, coarse, rho, *refs,
+):
+    tables, kept = refs[:7], refs[10:17]
+    copies = [pltpu.make_async_copy(a, b, refs[17].at[i]) for i, (a, b) in enumerate(zip(tables, kept))]
+    run(subs, slabs, rows, width, source, coarse, rho, copies, *kept, *refs[7:10], *refs[18:])
+
+
+def run(
+    subs, slabs, rows, width, source, coarse, rho, copies,
+    basis_x, basis_y, basis_z, eigen_x, eigen_y, eigen_z, stiff,
     solved, own_mult, own_jump,
     source_in, coarse_in, sent, lines, spread, got,
     z_right, zt_right, yt_left, xt_left, x_left, x_t, y_t, stiff_t,
@@ -88,6 +99,7 @@
             copy.start()
 
     start(fetch(1, 0, 0))
+    start([copies[2], copies[1]])
 
     barrier = pltpu.get_barrier_semaphore()
     for m in range(1, slabs):
@@ -95,7 +107,10 @@
     for m in range(1, subs):
         pl.semaphore_signal(barrier, inc=1, device_id=(lax.rem(sub + m, subs), me), device_id_type=MESH)
 
+    start(copies[at] for at in (0, 3, 4, 5, 6))
+    copies[2].wait()
     z_right[...] = as_right(basis_z[...])
+    copies[1].wait()
     y_t[...] = basis_y[...].T
     yt_left[...] = as_left(y_t[...])
 
@@ -146,6 +161,8 @@
         keep(c).start()
 
     start(fetch(0, 0, 0))
+    for at in (0, 3, 4, 5, 6):
+        copies[at].wait()
     square = lambda row: jnp.broadcast_to(row, (width, width))
     down = lambda row: square(row).T
     y_column = down(eigen_y[...])
@@ -165,8 +182,7 @@
         y_parts[c] = padded(own_y, True).T.astype(BF16)
 
     transform(0, spread, lambda g: None)
-    quarter = rows // 4
-    rest = [(c, q * quarter, quarter) for c in range(2, chunks) for q in range(4)]
+    rest = [(c, q * rows // 4, rows // 4) for c in range(2, chunks) for q in range(4)]
     for piece in rest[:1]:
         forward_all(*piece)
 
@@ -302,7 +318,9 @@
         lax.fori_loop(0, TILE, one, 0)
 
     last = chunks - 1
-    quarters = [pl.ds(q * quarter * step_rows, quarter * step_rows) for q in range(4)]
+    pieces = PIECES
+    quarter = rows // pieces
+    quarters = [pl.ds(q * quarter * step_rows, quarter * step_rows) for q in range(pieces)]
 
     def inverse(c, m, q=None):
         d = ahead(m)
@@ -322,7 +340,7 @@
     back = []
 
     def give(c):
-        copies = [inverse(c, m, q) for q in (range(4) if c == last else [None]) for m in range(1, slabs)]
+        copies = [inverse(c, m, q) for q in (range(pieces) if c == last else [None]) for m in range(1, slabs)]
         start(copies)
         back.extend(copies)
 
@@ -354,33 +372,15 @@
         give(c)
 
     def finish(c, q):
-        def depth(d, carry):
-            whole = got[c * slabs + d, quarters_at(q), :].reshape(quarter, halves, TILE, lanes)
-            whole = jnp.concatenate([whole[:, h].reshape(quarter * TILE, lanes) for h in range(halves)], axis=1)
-            whole = dot(as_left(whole), zt_right[...])
-            whole = [whole[:, h * lanes : (h + 1) * lanes].reshape(quarter, 1, TILE, lanes) for h in range(halves)]
-            got[c * slabs + d, quarters_at(q), :] = jnp.concatenate(whole, axis=1).reshape(quarter * step_rows, lanes)
-            return carry
-
-        lax.fori_loop(0, slabs, depth, 0)
-
-        def across(r, carry):
+        at = pl.ds(pl.multiple_of(q * quarter * step_rows, TILE), quarter * step_rows)
+        whole = got[pl.ds(c * slabs, slabs), at, :].reshape(slabs * quarter, halves, TILE, lanes)
+        whole = [whole[:, h].reshape(slabs * quarter * TILE, lanes) for h in range(halves)]
+        whole = dot(as_left(jnp.concatenate(whole, axis=1)), zt_right[...])
+        whole = whole.reshape(slabs, quarter, TILE, width)
+        for r in range(quarter):
+            part = dot(y_parts[c], padded(whole[:, r].reshape(slabs * TILE, width), False).astype(BF16))
             x = q * quarter + r
-            at = [pl.ds(pl.multiple_of(x * step_rows + h * TILE, TILE), TILE) for h in range(halves)]
-            right = jnp.concatenate(
-                [
-                    jnp.concatenate([got[c * slabs + d, at[h], :] for d in range(slabs)], axis=0)
-                    for h in range(halves)
-                ],
-                axis=1,
-            )
-            part = dot(y_parts[c], padded(right, False).astype(BF16))
             solved[x] = part if c == 0 else solved[x] + part
-            return carry
-
-        lax.fori_loop(0, quarter, across, 0)
-
-    quarters_at = lambda q: pl.ds(pl.multiple_of(q * quarter * step_rows, TILE), quarter * step_rows)
 
     def arrive(c):
         stay(c).wait()
@@ -392,9 +392,9 @@
                 finish(c, q)
                 return carry
 
-            lax.fori_loop(0, 4, one, 0)
+            lax.fori_loop(0, pieces, one, 0)
         else:
-            for q in range(4):
+            for q in range(pieces):
                 for m in range(1, slabs):
                     inverse_from(c, m, q).wait_recv()
                 finish(c, q)
@@ -457,6 +457,7 @@
     half = slabs // 2
     stack = 3 * slabs * TILE
     stack += -stack % LANES
+    line = pltpu.VMEM((1, width), F32)
     dma = pltpu.SemaphoreType.DMA
     vmem = pl.BlockSpec(memory_space=pltpu.VMEM)
     hbm = pl.BlockSpec(memory_space=pl.ANY)
@@ -467,9 +468,10 @@
             pltpu.VMEM((rows, width), F32),
             pltpu.VMEM((rows, width), F32),
         ),
-        in_specs=[hbm, hbm, pl.BlockSpec(memory_space=pltpu.SMEM)] + [vmem] * 7,
+        in_specs=[hbm, hbm, pl.BlockSpec(memory_space=pltpu.SMEM)] + [hbm] * 7,
         out_specs=(vmem, vmem, vmem),
         scratch_shapes=[
+            face(), face(), face(), line, line, line, face(), dma((7,)),
             face(2, GROUP), face(2, GROUP), field(), field(), field(), field(),
             pltpu.VMEM((3 * width, width), BF16), pltpu.VMEM((3 * width, width), BF16),
             pltpu.VMEM((width, 3 * width), BF16), pltpu.VMEM((width, 3 * width), BF16),
@@ -482,7 +484,7 @@
             pltpu.VMEM((ITERS, TILE, LANES), F32), pltpu.VMEM((ITERS, subs, TILE, LANES), F32),
             dma((2, 2)), dma((chunks,)),
             dma((chunks, slabs)), dma((chunks, slabs)), dma((chunks, slabs)), dma((chunks, slabs)),
-            dma((4, slabs)), dma((4, slabs)),
+            dma((PIECES, slabs)), dma((PIECES, slabs)),
             dma((half,)), dma((half,)), dma((2,)), dma((2,)), dma((3, half)), dma((3, half)),
             dma((3,)), dma((3,)), dma((ITERS, subs)), dma((ITERS, subs)),
         ],
@@ -491,6 +493,34 @@
         ),
         name="feti",
     )(source, coarse, rho, basis_x, basis_y, basis_z, eigen_x, eigen_y, eigen_z, stiff)
+
+
+def hand_out_kernel(*refs):
+    count = len(refs) // 2
+    copies = []
+    for i in range(count):
+        parts = min(HAND_OUT, refs[i].shape[0]) if i == 0 else 1
+        lot = refs[i].shape[0] // parts
+        for part in range(parts):
+            at = pl.ds(part * lot, lot)
+            copies.append(pltpu.make_async_copy(refs[i].at[at], refs[count + i].at[at], refs[-1].at[len(copies)]))
+    for copy in copies:
+        copy.start()
+    for copy in copies:
+        copy.wait()
+
+
+def hand_out(*results):
+    anywhere = pl.BlockSpec(memory_space=pl.ANY)
+    return pl.pallas_call(
+        hand_out_kernel,
+        out_shape=[pltpu.HBM(value.shape, value.dtype) for value in results],
+        in_specs=[anywhere] * len(results),
+        out_specs=[anywhere] * len(results),
+        scratch_shapes=[pltpu.SemaphoreType.DMA((HAND_OUT + len(results),))],
+        compiler_params=pltpu.CompilerParams(vmem_limit_bytes=2**20),
+        name="hand_out",
+    )(*(pltpu.with_memory_space_constraint(value, pltpu.VMEM) for value in results))
 
 
 def on_device(
@@ -502,6 +532,7 @@
         subs, slabs, source, coarse, rho, basis_x, basis_y, basis_z,
         eigen_x[None], eigen_y[None], eigen_z[None], face_stiff,
     )
+    solved, multipliers, jump = hand_out(solved, multipliers, jump)
     return (solved[None], multipliers[None], jump[None])
 
 

time: 383 us -> 380 us (level)
  local copies, waits for them, and re-layouts: 4.63 us -> 0 us
    unnamed x3 -> x0, local copies, waits for them, and re-layouts: 4.63 us -> none
where the time goes in v3:
time: 380 us; the launch traced here: 379 us
  Pallas kernels  378 us (99%)
    pallas_call x1, Pallas kernels, iterate(): pl.pallas_call(functools.partial(feti_kernel, subs, slabs, rows, width),...  374 us

profile of v3, /device:TPU:8, one launch (start us, length us, event | category | flops | bytes accessed | tf_op | source)
XLA Modules:
  0.0 378.6 jit_solution(6161929454177754383)
XLA Ops:
  0.6 374.4 %feti.1 = (f32[32,256,256]{2,1,0:T(8,128)S(1)}, f32[32,256]{1,0:T(8,128)S(1)}, f32[32,256]{1,0:T(8,128)S(1)}) custom-call(f32[1,32,256,256]{3,2,1,0:T(8,128)} %source.1, f32[2,1,32,256,256]{4,3,2,1,0:T(8,128)} %coarse.1, f32[4]{0:T(128)} %rho.1, f32[256,256]{1,0:T(8,128)} %refs_0_.1, f32[256,256]{1,0:T(8,128)} %refs_1_.1, f32[256,256]{1,0:T(8,128)} %refs_2_.1, ...), custom_call_target="tpu_custom_call" | custom-call | tf_op jit(solution)/shard_map/feti/pallas_call | solution.py:464
  375.0 3.4 hand_out.1

commit v4 on v3

--- a/solution.py
+++ b/solution.py
@@ -9,7 +9,7 @@
 
 ITERS = 2
 GROUP = 2
-PIECES = 8
+PIECES = 4
 HAND_OUT = 8
 TILE = 8
 LANES = 128
@@ -114,8 +114,6 @@
     y_t[...] = basis_y[...].T
     yt_left[...] = as_left(y_t[...])
 
-    pl.semaphore_wait(barrier, slabs + subs - 2)
-
     def forward(m, c, first, count):
         at = pl.ds(first * step_rows, count * step_rows)
         d = ahead(m)
@@ -128,7 +126,7 @@
         for m in range(1, slabs):
             forward(m, c, first, count).start()
 
-    def transform(which, store, after):
+    def transform(which, store):
         steps = rows // GROUP
 
         def step(g, carry):
@@ -147,12 +145,21 @@
                 for h in range(halves):
                     at = pl.ds(pl.multiple_of((g * GROUP + r) * step_rows + h * TILE, TILE), TILE)
                     store[:, at, :] = part[:, h * lanes : (h + 1) * lanes].reshape(width // TILE, TILE, lanes)
-            after(g)
             return carry
 
-        lax.fori_loop(0, steps, step, 0)
-
-    transform(1, sent, lambda g: forward_all(0, g * GROUP, GROUP))
+        return steps, step
+
+    steps, step = transform(1, sent)
+    step(0, 0)
+    pl.semaphore_wait(barrier, slabs + subs - 2)
+    forward_all(0, 0, GROUP)
+
+    def step_and_send(g, carry):
+        step(g, carry)
+        forward_all(0, g * GROUP, GROUP)
+        return carry
+
+    lax.fori_loop(1, steps, step_and_send, 0)
     if chunks > 1:
         forward_all(1, 0, rows)
 
@@ -181,7 +188,7 @@
         own_y = jnp.concatenate([y_t[d * rows + c * TILE : d * rows + (c + 1) * TILE, :] for d in range(slabs)], axis=0)
         y_parts[c] = padded(own_y, True).T.astype(BF16)
 
-    transform(0, spread, lambda g: None)
+    lax.fori_loop(0, *transform(0, spread), 0)
     rest = [(c, q * rows // 4, rows // 4) for c in range(2, chunks) for q in range(4)]
     for piece in rest[:1]:
         forward_all(*piece)

time: 380 us -> 379 us (level)
  no operation moved by 1% of the time
where the time goes in v4:
time: 379 us; the launch traced here: 378 us
  Pallas kernels  377 us (99%)
    pallas_call x1, Pallas kernels, iterate(): pl.pallas_call(functools.partial(feti_kernel, subs, slabs, rows, width),...  374 us

profile of v4, /device:TPU:8, one launch (start us, length us, event | category | flops | bytes accessed | tf_op | source)
XLA Modules:
  0.0 377.9 jit_solution(7068646886430087271)
XLA Ops:
  0.6 373.7 %feti.1 = (f32[32,256,256]{2,1,0:T(8,128)S(1)}, f32[32,256]{1,0:T(8,128)S(1)}, f32[32,256]{1,0:T(8,128)S(1)}) custom-call(f32[1,32,256,256]{3,2,1,0:T(8,128)} %source.1, f32[2,1,32,256,256]{4,3,2,1,0:T(8,128)} %coarse.1, f32[4]{0:T(128)} %rho.1, f32[256,256]{1,0:T(8,128)} %refs_0_.1, f32[256,256]{1,0:T(8,128)} %refs_1_.1, f32[256,256]{1,0:T(8,128)} %refs_2_.1, ...), custom_call_target="tpu_custom_call" | custom-call | tf_op jit(solution)/shard_map/feti/pallas_call | solution.py:471
  374.4 3.4 hand_out.1

commit v5 on v4

--- a/solution.py
+++ b/solution.py
@@ -347,7 +347,7 @@
     back = []
 
     def give(c):
-        copies = [inverse(c, m, q) for q in (range(pieces) if c == last else [None]) for m in range(1, slabs)]
+        copies = [inverse(c, m, q) for q in (range(pieces) if c == last else [None]) for m in range(slabs - 1, 0, -1)]
         start(copies)
         back.extend(copies)
 

time: 379 us -> 382 us (level); the launches traced: 378 us -> 377 us
  no operation moved by 1% of the time
where the time goes in v5:
time: 382 us; the launch traced here: 377 us
  Pallas kernels  376 us (98%)
    pallas_call x1, Pallas kernels, iterate(): pl.pallas_call(functools.partial(feti_kernel, subs, slabs, rows, width),...  372 us

profile of v5, /device:TPU:8, one launch (start us, length us, event | category | flops | bytes accessed | tf_op | source)
XLA Modules:
  0.0 376.6 jit_solution(12732023265102269647)
XLA Ops:
  0.6 372.4 %feti.1 = (f32[32,256,256]{2,1,0:T(8,128)S(1)}, f32[32,256]{1,0:T(8,128)S(1)}, f32[32,256]{1,0:T(8,128)S(1)}) custom-call(f32[1,32,256,256]{3,2,1,0:T(8,128)} %source.1, f32[2,1,32,256,256]{4,3,2,1,0:T(8,128)} %coarse.1, f32[4]{0:T(128)} %rho.1, f32[256,256]{1,0:T(8,128)} %refs_0_.1, f32[256,256]{1,0:T(8,128)} %refs_1_.1, f32[256,256]{1,0:T(8,128)} %refs_2_.1, ...), custom_call_target="tpu_custom_call" | custom-call | tf_op jit(solution)/shard_map/feti/pallas_call | solution.py:471
  373.0 3.4 hand_out.1
